TPU v7x, 32 devices: a whole 2x2x4 slice. The times are simulated.
32 devices in a mesh: dp: 8 (over y, x, core), mp: 4 (over z).
Axes of the slice: x: 2, y: 2, z: 4, core: 2. Of those that a mesh axis runs over, the one named last changes fastest.
Arguments:
- ref_hidden: bfloat16 [512, 2048], P('dp', 'mp'), may hold values from -80 to 80
- proxy_hidden: bfloat16 [512, 2048], P('dp', 'mp'), may hold values from -80 to 80
- ref_gain: float32 [2048], replicated, may hold values from 0.5 to 1.5
- proxy_gain: float32 [2048], replicated, may hold values from 0.5 to 1.5
- ref_head: bfloat16 [2048, 128256], P(None, ('dp', 'mp')), may hold values from -16 to 16
- proxy_head: bfloat16 [2048, 128256], P(None, ('dp', 'mp')), may hold values from -16 to 16
- token_ids: int32 [512], P('dp'), may hold values from 0 to 128255
- bucket_ids: int32 [512], P(('dp', 'mp')), may hold values from 0 to 4095
- domain_of_bucket: int32 [4096], replicated, may hold values from 0 to 21
- prior_weights: float32 [22], replicated, may hold values from 0.01 to 0.1
Outputs:
- ref_loss: float32 [512], P(('dp', 'mp'))
- proxy_loss: float32 [512], P(('dp', 'mp'))
- bucket_excess: float32 [4096], P(('dp', 'mp'))
- domain_log_weights: float32 [22], replicated
All inputs are finite; a program needn't handle non-finite values.
Results may differ from a plain program's by a relative error of at most 0.0035.
Values may be sent and summed in bfloat16 or wider, within the bound.
No kernel may reach another device: no remote copies, remote signals or barrier semaphores. Data moves between devices by JAX's collectives and lax.ppermute only.
A program may use at most 128 MiB of HBM per device.

v0:
```python
import jax
import jax.numpy as jnp
from jax import lax
from jax.sharding import PartitionSpec as P


def normalize(hidden, gain):
    values = hidden.astype(jnp.float32)
    scale = lax.rsqrt(jnp.mean(values * values, -1, keepdims=True) + 1e-05)
    return (values * scale * gain).astype(jnp.bfloat16)


def row_stats(normed, targets, head, offset):
    logits = jnp.dot(normed, head, preferred_element_type=jnp.float32)
    top = jnp.max(logits, -1)
    total = jnp.sum(jnp.exp(logits - top[:, None]), -1)
    columns = lax.broadcasted_iota(jnp.int32, logits.shape, 1) + offset
    target = jnp.sum(jnp.where(columns == targets[:, None], logits, 0.0), -1)
    return (top, total, target)


def both_stats(norm_ref, norm_proxy, targets, ref_head, proxy_head, offset):
    first = row_stats(norm_ref, targets, ref_head, offset)
    second = row_stats(norm_proxy, targets, proxy_head, offset)
    return tuple((jnp.stack([left, right]) for left, right in zip(first, second)))


def on_device(
    ref_hidden,
    proxy_hidden,
    ref_gain,
    proxy_gain,
    ref_head,
    proxy_head,
    token_ids,
    bucket_ids,
    domain_of_bucket,
    prior_weights,
):
    vocab_dev = ref_head.shape[1]
    device = lax.axis_index(("dp", "mp"))
    offset = device * vocab_dev
    own_rows = bucket_ids.shape[0]
    full_ref, full_proxy = (
        lax.all_gather(ref_hidden, "mp", axis=1, tiled=True),
        lax.all_gather(proxy_hidden, "mp", axis=1, tiled=True),
    )
    norm_ref = normalize(full_ref, ref_gain)
    norm_proxy = normalize(full_proxy, proxy_gain)
    stats = both_stats(
        lax.all_gather(norm_ref, "dp", axis=0, tiled=True),
        lax.all_gather(norm_proxy, "dp", axis=0, tiled=True),
        lax.all_gather(token_ids, "dp", axis=0, tiled=True),
        ref_head,
        proxy_head,
        offset,
    )
    top, total, target = tuple((fresh for fresh in stats))
    first_row = device * own_rows
    whole_top = lax.pmax(top, ("dp", "mp"))
    terms = jnp.concatenate([total * jnp.exp(top - whole_top), target], 0)
    shares = lax.psum_scatter(terms, ("dp", "mp"), scatter_dimension=1, tiled=True)
    own_top = lax.dynamic_slice_in_dim(whole_top, first_row, own_rows, 1)
    own_total = shares[:2]
    own_target = shares[2:]
    losses = own_top + jnp.log(own_total) - own_target
    excess = jnp.maximum(losses[1] - losses[0], 0.0)
    buckets = domain_of_bucket.shape[0]
    domains = prior_weights.shape[0]
    onehot = (bucket_ids[:, None] == lax.broadcasted_iota(jnp.int32, (1, buckets), 1)).astype(
        jnp.float32
    )
    table = jnp.dot(
        jnp.stack([excess, jnp.ones_like(excess)]),
        onehot,
        precision=lax.Precision.HIGHEST,
        preferred_element_type=jnp.float32,
    )
    domain_hot = (
        domain_of_bucket[:, None] == lax.broadcasted_iota(jnp.int32, (1, domains), 1)
    ).astype(jnp.float32)
    bucket_dev = buckets // lax.axis_size(("dp", "mp"))
    first_bucket = device * bucket_dev
    full_table = lax.psum(table, ("dp", "mp"))
    domain_totals = jnp.dot(
        full_table, domain_hot, precision=lax.Precision.HIGHEST, preferred_element_type=jnp.float32
    )
    own_table = lax.dynamic_slice_in_dim(full_table, first_bucket, bucket_dev, 1)
    bucket_excess = own_table[0] / jnp.maximum(own_table[1], 1.0)
    domain_excess = domain_totals[0] / jnp.maximum(domain_totals[1], 1.0)
    weights = jax.nn.softmax(jnp.log(prior_weights) + 1.0 * domain_excess)
    domain_log_weights = jnp.log(0.999 * weights + 0.001 / domains)
    return (losses[0], losses[1], bucket_excess, domain_log_weights)


def solution(mesh):
    placed = (
        P("dp", "mp"),
        P("dp", "mp"),
        P(),
        P(),
        P(None, ("dp", "mp")),
        P(None, ("dp", "mp")),
        P("dp"),
        P(("dp", "mp")),
        P(),
        P(),
    )
    return jax.shard_map(
        on_device,
        mesh=mesh,
        in_specs=placed,
        out_specs=(P(("dp", "mp")), P(("dp", "mp")), P(("dp", "mp")), P()),
        check_vma=False,
    )
```

profile of v0, /device:TPU:12, one launch (start us, length us, event | category | flops | bytes accessed | tf_op | source)
XLA Modules:
  0.0 333.8 jit_solution(15853292360239945124)
XLA Ops:
  7.2 0.0 all-gather.5.cloned.1.call-start
  7.2 14.8 %all_gather.17 = bf16[64,2048]{1,0:T(8,128)(2,1)S(1)} all-gather(bf16[64,512]{1,0:T(8,128)(2,1)} %param.11), channel_id=1, replica_groups=mesh['dp'=8,'mp'=4] {'mp'}, dimensions={1}, use_global_device_ids=true | all-gather | bytes 327680 | tf_op jit(solution)/shard_map/all_gather | solution.py:46
  22.0 0.2 fusion.5
  22.2 1.5 fusion.7
  23.7 0.0 all-gather.5.cloned.1.call-update
  23.8 0.0 all-gather.3.cloned.1.call-start
  23.8 14.1 %all_gather.15 = bf16[64,2048]{1,0:T(8,128)(2,1)S(1)} all-gather(bf16[64,512]{1,0:T(8,128)(2,1)} %param.10), channel_id=1, replica_groups=mesh['dp'=8,'mp'=4] {'mp'}, dimensions={1}, use_global_device_ids=true | all-gather | bytes 327680 | tf_op jit(solution)/shard_map/all_gather | solution.py:45
  37.9 0.2 fusion.2
  38.1 1.5 fusion.4
  39.6 0.0 all-gather.3.cloned.1.call-update
  39.6 0.0 reduce-scatter.4.cloned.1.call-start
  39.7 1.2 dynamic-slice
  41.6 0.9 dynamic-update-slice
  42.4 7.4 %all-reduce.1 = s32[512]{0:T(512)S(1)} all-reduce(s32[512]{0:T(512)S(1)} %dynamic-update-slice), channel_id=1, replica_groups=mesh['dp'=8,'mp'=4] {'dp'}, use_global_device_ids=true, to_apply=%add.1 | all-reduce | flops 512 | bytes 4096
  49.8 3.0 all-gather.5.cloned.1.call-done
  52.8 14.5 %fusion.19 = (f32[512]{0:T(512)S(1)}, f32[512,4008]{0,1:T(8,128)}) fusion(bf16[512,2048]{1,0:T(8,128)(2,1)} %all-gather.5.cloned.1.call-done, bf16[2048,4008]{0,1:T(8,128)(2,1)} %param.15), kind=kOutput, calls=%fused_computation.45 | convolution fusion | flops 8407436800 | bytes 26724352 | tf_op jit(solution)/shard_map/dot_general | solution.py:14
  67.3 15.1 %all-gather.3.cloned.1.call-done = bf16[512,2048]{1,0:T(8,128)(2,1)} async-done(((bf16[64,2048]{1,0:T(8,128)(2,1)}), bf16[512,2048]{1,0:T(8,128)(2,1)}) %all-gather.3.cloned.1.call-update) | async-done | bytes 2097168 | tf_op jit(solution)/shard_map/all_gather | solution.py:51
  82.5 14.4 %fusion.18 = (f32[512]{0:T(512)S(1)}, f32[512,4008]{0,1:T(8,128)}) fusion(bf16[512,2048]{1,0:T(8,128)(2,1)} %all-gather.3.cloned.1.call-done, bf16[2048,4008]{0,1:T(8,128)(2,1)} %param.14), kind=kOutput, calls=%fused_computation.44 | convolution fusion | flops 8407436800 | bytes 26724352 | tf_op jit(solution)/shard_map/dot_general | solution.py:14
  96.8 40.1 %pmax.7 = f32[2,512]{1,0:T(2,128)S(1)} all-reduce(f32[2,512]{1,0:T(2,128)S(1)} %pad_maximum_fusion.1), channel_id=1, replica_groups=mesh['dp'=8,'mp'=4] {'dp','mp'}, use_global_device_ids=true, to_apply=%region_4.5 | all-reduce | flops 1024 | bytes 8192 | tf_op jit(solution)/shard_map/pmax | solution.py:60
  137.0 0.0 copy-start.2
  137.0 0.0 copy-start.1
  137.0 0.0 copy-start
  137.0 7.9 %exponential_reduce_fusion.1 = (f32[512]{0:T(512)S(1)}, f32[512]{0:T(512)S(1)}, f32[512]{0:T(512)S(1)}, f32[512]{0:T(512)S(1)}) fusion(f32[512,4008]{0,1:T(8,128)} %get-tuple-element.18, f32[512]{0:T(512)S(1)} %get-tuple-element.17, s32[512]{0:T(512)S(1)} %all-reduce.1, s32[4008]{0:T(1024)S(1)} %iota_add_fusion, f32[512,4008]{0,1:T(8,128)} %get-tuple-element.20, ...), kind=kLoop, calls=%fused_computation.5 | loop fusion | flops 18466816 | bytes 16447136 | tf_op jit(solution)/shard_map/reduce_sum | solution.py:16
  144.9 0.8 copy.14
  145.8 0.0 reduce-scatter.4.cloned.1.call-update
  145.8 131.7 %reduce-scatter.4.cloned.1.call-done = f32[16,4]{1,0:T(8,128)} async-done(((f32[512,4]{1,0:T(8,128)}), f32[16,4]{1,0:T(8,128)}) %reduce-scatter.4.cloned.1.call-update) | async-done | bytes 272
  277.5 0.8 fusion.17
  278.4 0.1 copy.16
  278.5 0.1 copy.17
  278.5 0.1 add_subtract_fusion
  278.6 0.5 subtract_maximum_fusion
  279.1 0.0 copy-done.2
  279.1 0.3 fusion.9
  279.4 43.2 %psum.7 = f32[2,4096]{1,0:T(2,128)S(1)} all-reduce(f32[2,4096]{1,0:T(2,128)S(1)} %fusion.9), channel_id=1, replica_groups=mesh['dp'=8,'mp'=4] {'dp','mp'}, use_global_device_ids=true, to_apply=%region_10.11 | all-reduce | flops 8192 | bytes 65536 | tf_op jit(solution)/shard_map/psum | solution.py:84
  322.6 0.0 copy-done.1
  322.6 0.3 fusion.8
  322.9 0.0 copy-done
  322.9 0.6 fusion.16
  323.6 1.3 fusion.15
  324.9 1.9 add_log_fusion
  326.8 0.5 fusion.13
  (8 shorter events, 0.1 us)
Async XLA Ops:
  7.2 45.6 %all-gather.5.cloned.1.call-start = ((), (), s32[]{:S(2)}) async-start(), calls=%async_computation.2 | async-start | bytes 2359296 | tf_op jit(solution)/shard_map/all_gather | solution.py:52
  23.8 58.7 %all-gather.3.cloned.1.call-start = ((), (), s32[]{:S(2)}) async-start(), calls=%async_computation.1 | async-start | bytes 2359296 | tf_op jit(solution)/shard_map/all_gather | solution.py:51
  39.6 237.9 %reduce-scatter.4.cloned.1.call-start = ((), (), s32[]{:S(2)}) async-start(), calls=%async_computation.3 | async-start | bytes 270336
  137.0 142.1 %copy-start.2 = (s32[16]{0:T(128)S(1)}, s32[16]{0:T(128)}, u32[]{:S(2)}) copy-start(s32[16]{0:T(128)} %param.17) | copy-start | bytes 196
  137.0 185.6 %copy-start.1 = (s32[4096]{0:T(1024)S(1)}, s32[4096]{0:T(1024)}, u32[]{:S(2)}) copy-start(s32[4096]{0:T(1024)} %param.18) | copy-start | bytes 49156
  137.0 185.9 %copy-start = (f32[22]{0:T(128)S(1)}, f32[22]{0:T(128)}, u32[]{:S(2)}) copy-start(f32[22]{0:T(128)} %param.19) | copy-start | bytes 268
Sparse Core Ops, SparseCore 0:
  23.9 28.8 all-gather.4
  54.7 27.7 all-gather.2
  145.9 131.5 reduce-scatter.3
where the time goes:
time: 335 us; the launch traced here: 334 us
  waiting for transfers between devices  150 us (45%)
  blocking collectives  120 us (36%)
  matrix products  29.5 us (9%)
  other arithmetic  16.3 us (5%)
  between operations  14.5 us (4%)
  local copies, waits for them, and re-layouts  3.97 us (1%)
    unnamed x4, waiting for transfers between devices  132 us
    psum x1, blocking collectives, on_device(): full_table = lax.psum(table, ('dp', 'mp'))  43.2 us
    pmax x1, blocking collectives, on_device(): whole_top = lax.pmax(top, ('dp', 'mp'))  40.1 us
    dot_general x2, matrix products, row_stats(): logits = jnp.dot(normed, head, preferred_element_type=jnp.float32)  28.9 us
    all_gather x1, waiting for transfers between devices, on_device(): lax.all_gather(norm_ref, 'dp', axis=0, tiled=True)  15.1 us
    all_gather x1, blocking collectives, on_device(): lax.all_gather(proxy_hidden, 'mp', axis=1, tiled=True)  14.8 us
    all_gather x1, blocking collectives, on_device(): lax.all_gather(ref_hidden, 'mp', axis=1, tiled=True)  14.1 us
    reduce_sum x1, other arithmetic, row_stats(): total = jnp.sum(jnp.exp(logits - top[:, None]), -1)  7.88 us
  transfers between devices with their start and end apart: 3, of which 3 were waited for; matrix products, arithmetic and copies ran while one was open for 5% of the time, Pallas kernels for 0%

commit v1 on v0

--- a/solution.py
+++ b/solution.py
@@ -81,7 +81,7 @@
     ).astype(jnp.float32)
     bucket_dev = buckets // lax.axis_size(("dp", "mp"))
     first_bucket = device * bucket_dev
-    full_table = lax.psum(table, ("dp", "mp"))
+    full_table = jnp.sum(lax.all_gather(table, ("dp", "mp")), axis=0)
     domain_totals = jnp.dot(
         full_table, domain_hot, precision=lax.Precision.HIGHEST, preferred_element_type=jnp.float32
     )

time: 335 us -> 350 us (1.045)
  waiting for transfers between devices: 150 us -> 204 us
  blocking collectives: 120 us -> 76.4 us
    all_gather x0 -> x1, waiting for transfers between devices: none -> 53.8 us  [on_device(): full_table = jnp.sum(lax.all_gather(table, ('dp', 'mp')), axis=0)]
    psum x1 -> x0, blocking collectives: 43.2 us -> none  [on_device(): full_table = lax.psum(table, ('dp', 'mp'))]
    unnamed x4 -> x5, waiting for transfers between devices: 132 us -> 132 us
  transfers between devices with their start and end apart: 3 -> 4, of which waited for: 3 -> 4; matrix products, arithmetic and copies ran while one was open for 5% -> 5% of each run, Pallas kernels for 0% -> 0%
where the time goes in v1:
time: 350 us; the launch traced here: 347 us
  waiting for transfers between devices  204 us (58%)
  blocking collectives  76.4 us (22%)
  matrix products  30.1 us (9%)
  other arithmetic  17.8 us (5%)
  between operations  14.5 us (4%)
  local copies, waits for them, and re-layouts  3.97 us (1%)
    unnamed x5, waiting for transfers between devices  132 us
    all_gather x1, waiting for transfers between devices, on_device(): full_table = jnp.sum(lax.all_gather(table, ('dp', 'mp')), axis=0)  53.8 us
    pmax x1, blocking collectives, on_device(): whole_top = lax.pmax(top, ('dp', 'mp'))  40.2 us
    dot_general x2, matrix products, row_stats(): logits = jnp.dot(normed, head, preferred_element_type=jnp.float32)  28.9 us
    all_gather x1, waiting for transfers between devices, on_device(): lax.all_gather(norm_ref, 'dp', axis=0, tiled=True)  15.1 us
    all_gather x1, blocking collectives, on_device(): lax.all_gather(proxy_hidden, 'mp', axis=1, tiled=True)  14.8 us
    all_gather x1, blocking collectives, on_device(): lax.all_gather(ref_hidden, 'mp', axis=1, tiled=True)  14.1 us
    reduce_sum x1, other arithmetic, row_stats(): total = jnp.sum(jnp.exp(logits - top[:, None]), -1)  7.88 us
  transfers between devices with their start and end apart: 4, of which 4 were waited for; matrix products, arithmetic and copies ran while one was open for 5% of the time, Pallas kernels for 0%

profile of v1, /device:TPU:12, one launch (start us, length us, event | category | flops | bytes accessed | tf_op | source)
XLA Modules:
  0.0 346.6 jit_solution(574501351042035951)
XLA Ops:
  7.2 0.0 all-gather.8.cloned.1.call-start
  7.2 14.8 %all_gather.23 = bf16[64,2048]{1,0:T(8,128)(2,1)S(1)} all-gather(bf16[64,512]{1,0:T(8,128)(2,1)} %param.11), channel_id=1, replica_groups=mesh['dp'=8,'mp'=4] {'mp'}, dimensions={1}, use_global_device_ids=true | all-gather | bytes 327680 | tf_op jit(solution)/shard_map/all_gather | solution.py:46
  22.0 0.2 fusion.5
  22.2 1.5 fusion.7
  23.7 0.0 all-gather.8.cloned.1.call-update
  23.8 0.0 all-gather.6.cloned.1.call-start
  23.8 14.1 %all_gather.21 = bf16[64,2048]{1,0:T(8,128)(2,1)S(1)} all-gather(bf16[64,512]{1,0:T(8,128)(2,1)} %param.10), channel_id=1, replica_groups=mesh['dp'=8,'mp'=4] {'mp'}, dimensions={1}, use_global_device_ids=true | all-gather | bytes 327680 | tf_op jit(solution)/shard_map/all_gather | solution.py:45
  37.9 0.2 fusion.2
  38.1 1.5 fusion.4
  39.6 0.0 all-gather.6.cloned.1.call-update
  39.6 0.0 reduce-scatter.4.cloned.1.call-start
  39.7 1.2 dynamic-slice
  41.6 0.9 dynamic-update-slice
  42.4 7.4 %all-reduce.1 = s32[512]{0:T(512)S(1)} all-reduce(s32[512]{0:T(512)S(1)} %dynamic-update-slice), channel_id=1, replica_groups=mesh['dp'=8,'mp'=4] {'dp'}, use_global_device_ids=true, to_apply=%add.1 | all-reduce | flops 512 | bytes 4096
  49.8 3.0 all-gather.8.cloned.1.call-done
  52.8 14.5 %fusion.18 = (f32[512]{0:T(512)S(1)}, f32[512,4008]{0,1:T(8,128)}) fusion(bf16[512,2048]{1,0:T(8,128)(2,1)} %all-gather.8.cloned.1.call-done, bf16[2048,4008]{0,1:T(8,128)(2,1)} %param.15), kind=kOutput, calls=%fused_computation.45 | convolution fusion | flops 8407436800 | bytes 26724352 | tf_op jit(solution)/shard_map/dot_general | solution.py:14
  67.3 15.1 %all-gather.6.cloned.1.call-done = bf16[512,2048]{1,0:T(8,128)(2,1)} async-done(((bf16[64,2048]{1,0:T(8,128)(2,1)}), bf16[512,2048]{1,0:T(8,128)(2,1)}) %all-gather.6.cloned.1.call-update) | async-done | bytes 2097168 | tf_op jit(solution)/shard_map/all_gather | solution.py:51
  82.5 14.4 %fusion.17 = (f32[512]{0:T(512)S(1)}, f32[512,4008]{0,1:T(8,128)}) fusion(bf16[512,2048]{1,0:T(8,128)(2,1)} %all-gather.6.cloned.1.call-done, bf16[2048,4008]{0,1:T(8,128)(2,1)} %param.14), kind=kOutput, calls=%fused_computation.44 | convolution fusion | flops 8407436800 | bytes 26724352 | tf_op jit(solution)/shard_map/dot_general | solution.py:14
  96.8 40.2 %pmax.7 = f32[2,512]{1,0:T(2,128)S(1)} all-reduce(f32[2,512]{1,0:T(2,128)S(1)} %pad_maximum_fusion.1), channel_id=1, replica_groups=mesh['dp'=8,'mp'=4] {'dp','mp'}, use_global_device_ids=true, to_apply=%region_4.5 | all-reduce | flops 1024 | bytes 8192 | tf_op jit(solution)/shard_map/pmax | solution.py:60
  137.0 0.0 copy-start.2
  137.0 0.0 copy-start.1
  137.0 0.0 copy-start
  137.0 7.9 %exponential_reduce_fusion.1 = (f32[512]{0:T(512)S(1)}, f32[512]{0:T(512)S(1)}, f32[512]{0:T(512)S(1)}, f32[512]{0:T(512)S(1)}) fusion(f32[512,4008]{0,1:T(8,128)} %get-tuple-element.18, f32[512]{0:T(512)S(1)} %get-tuple-element.17, s32[512]{0:T(512)S(1)} %all-reduce.1, s32[4008]{0:T(1024)S(1)} %iota_add_fusion, f32[512,4008]{0,1:T(8,128)} %get-tuple-element.20, ...), kind=kLoop, calls=%fused_computation.5 | loop fusion | flops 18466816 | bytes 16447136 | tf_op jit(solution)/shard_map/reduce_sum | solution.py:16
  144.9 0.8 copy.14
  145.8 0.0 reduce-scatter.4.cloned.1.call-update
  145.8 0.0 all-gather.10.cloned.1.call-start
  145.9 131.7 %reduce-scatter.4.cloned.1.call-done = f32[16,4]{1,0:T(8,128)} async-done(((f32[512,4]{1,0:T(8,128)}), f32[16,4]{1,0:T(8,128)}) %reduce-scatter.4.cloned.1.call-update) | async-done | bytes 272
  277.5 0.8 fusion.16
  278.4 0.1 copy.16
  278.5 0.1 copy.17
  278.5 0.1 add_subtract_fusion
  278.6 0.5 subtract_maximum_fusion
  279.1 0.0 copy-done.2
  279.1 0.9 convolution_bitcast_fusion
  280.0 0.0 all-gather.10.cloned.1.call-update
  280.0 53.8 %all-gather.10.cloned.1.call-done = f32[32,2,4096]{2,1,0:T(2,128)} async-done(((f32[1,2,4096]{2,1,0:T(2,128)}), f32[32,2,4096]{2,1,0:T(2,128)}) %all-gather.10.cloned.1.call-update) | async-done | bytes 1048592 | tf_op jit(solution)/shard_map/all_gather | solution.py:84
  333.9 1.5 reduce_sum.78
  335.4 0.0 copy-done.1
  335.4 0.3 fusion.8
  335.7 0.0 copy-done
  335.7 0.6 fusion.15
  336.3 1.3 fusion.14
  337.7 1.9 add_log_fusion
  339.5 0.5 fusion.12
  (8 shorter events, 0.1 us)
Async XLA Ops:
  7.2 45.6 %all-gather.8.cloned.1.call-start = ((), (), s32[]{:S(2)}) async-start(), calls=%async_computation.2 | async-start | bytes 2359296 | tf_op jit(solution)/shard_map/all_gather | solution.py:52
  23.8 58.7 %all-gather.6.cloned.1.call-start = ((), (), s32[]{:S(2)}) async-start(), calls=%async_computation.1 | async-start | bytes 2359296 | tf_op jit(solution)/shard_map/all_gather | solution.py:51
  39.6 237.9 %reduce-scatter.4.cloned.1.call-start = ((), (), s32[]{:S(2)}) async-start(), calls=%async_computation.4 | async-start | bytes 270336
  137.0 142.1 %copy-start.2 = (s32[16]{0:T(128)S(1)}, s32[16]{0:T(128)}, u32[]{:S(2)}) copy-start(s32[16]{0:T(128)} %param.17) | copy-start | bytes 196
  137.0 198.4 %copy-start.1 = (s32[4096]{0:T(1024)S(1)}, s32[4096]{0:T(1024)}, u32[]{:S(2)}) copy-start(s32[4096]{0:T(1024)} %param.18) | copy-start | bytes 49156
  137.0 198.7 %copy-start = (f32[22]{0:T(128)S(1)}, f32[22]{0:T(128)}, u32[]{:S(2)}) copy-start(f32[22]{0:T(128)} %param.19) | copy-start | bytes 268
  145.8 188.0 %all-gather.10.cloned.1.call-start = ((), (), s32[]{:S(2)}) async-start(), calls=%async_computation.3 | async-start | bytes 1081344 | tf_op jit(solution)/shard_map/all_gather | solution.py:84
Sparse Core Ops, SparseCore 0:
  23.9 28.8 all-gather.7
  54.7 27.7 all-gather.5
  145.9 131.5 reduce-scatter.3
  280.4 53.4 all-gather.9
